TPU v7x, 32 devices: a whole 2x2x4 slice. The times are simulated.
32 devices in a mesh: tm: 16 (over z, y, x), body: 2 (over core).
Axes of the slice: x: 2, y: 2, z: 4, core: 2. Of those that a mesh axis runs over, the one named last changes fastest.
Arguments:
- states: float32 [16, 6, 2048], P('tm', None, 'body'), may hold values from -3 to 3, as said below
- masses: float32 [2048], P('body'), may hold values from 0.25 to 4
- frequency: float32 [2048], P('body'), may hold values from 0.35 to 1
Outputs:
- fine_end: float32 [16, 6, 2048], P('tm', None, 'body')
- correction: float32 [16, 6, 2048], P('tm', None, 'body')
- next_start: float32 [16, 6, 2048], P('tm', None, 'body')
Inputs may be any that keep to these rules, and one draw needn't show every extreme that they name: `states`: each body's distance from the z axis lies between 1 and 2 and its |z| is at most 0.2 in every slice's state.
All inputs are finite; a program needn't handle non-finite values.
Results may differ from a plain program's by a relative error of at most 0.0001.
Values sent between devices are 32-bit elements; how exact they have to be, the bound alone decides.
A program may use at most 64 MiB of HBM per device.

v0:
```python
import functools

import jax
import jax.numpy as jnp
from jax import lax
from jax.experimental import pallas as pl
from jax.experimental.pallas import tpu as pltpu
from jax.sharding import PartitionSpec as P

slice_time = 0.25
fine_step = 0.125
soften_sq = 0.01
disc_mass = 1.0

F32 = jnp.float32
BF16 = jnp.bfloat16
FEATURES = 48
SUM_ROWS = 32
TILE_I = 256


def group_size(count):
    best = 1
    for size in range(1, count + 1):
        if count % size == 0 and size * size <= count:
            best = size
    return best


def split3(value):
    high = value.astype(BF16).astype(F32)
    rest = value - high
    middle = rest.astype(BF16).astype(F32)
    return high, middle, rest - middle


def drift(planes, cos_turn, sin_turn, frequency):
    x, y, z, vx, vy, vz = planes
    return (
        cos_turn * x - sin_turn * y,
        sin_turn * x + cos_turn * y,
        cos_turn * z + sin_turn * vz / frequency,
        cos_turn * vx - sin_turn * vy,
        sin_turn * vx + cos_turn * vy,
        cos_turn * vz - sin_turn * frequency * z,
    )


def load_planes(ref):
    return tuple(ref[c] for c in range(6))


def store_planes(ref, planes):
    for c in range(6):
        ref[c] = planes[c]


def plane_sum(planes_a, planes_b):
    return sum(a * b for a, b in zip(planes_a, planes_b))


def kernel(
    nt, nb, g,
    state_hbm, mass_hbm, freq_hbm,
    out_hbm,
    state_ref, mass_ref, freq_ref, fine_ref, corr_ref, next_ref,
    feat, lhs, weigh, rhs_r, rhs_c, sum_s, sum_t,
    sendbuf, got, got_mass, grp, tot, carry_in,
    in_sem, out_sem,
    body_send, body_recv, mass_send, mass_recv,
    grp_send, grp_recv, tot_send, tot_recv,
):
    slot = lax.axis_index("tm")
    half = lax.axis_index("body")
    ng = nt // g
    q = slot // g
    r = slot % g
    chunks = state_ref.shape[1]
    lanes = chunks * 128
    wide = TILE_I // 128 if chunks % (TILE_I // 128) == 0 else 1
    mass_scale = disc_mass / (lanes * nb)

    barrier = pltpu.get_barrier_semaphore()
    for k in range(1, nb):
        pl.semaphore_signal(barrier, inc=1, device_id={"body": (half + k) % nb})
    for k in range(1, g):
        pl.semaphore_signal(barrier, inc=1, device_id={"tm": q * g + (r + k) % g})
    for k in range(1, ng):
        pl.semaphore_signal(barrier, inc=1, device_id={"tm": ((q + k) % ng) * g + r})
    arrivals = [
        pltpu.make_async_copy(src, dst, in_sem.at[n])
        for n, (src, dst) in enumerate(
            ((state_hbm, state_ref), (mass_hbm, mass_ref), (freq_hbm, freq_ref))
        )
    ]
    for copy in arrivals:
        copy.start()

    def body_copy(turn, k, src):
        return pltpu.make_async_remote_copy(
            src_ref=src, dst_ref=got.at[turn, k - 1],
            send_sem=body_send.at[turn, k - 1], recv_sem=body_recv.at[turn, k - 1],
            device_id={"body": (half + k) % nb},
        )

    def mass_copy(k):
        return pltpu.make_async_remote_copy(
            src_ref=mass_ref, dst_ref=got_mass.at[k - 1],
            send_sem=mass_send.at[k - 1], recv_sem=mass_recv.at[k - 1],
            device_id={"body": (half + k) % nb},
        )

    def pieces(planes):
        split = [split3(c) for c in planes]
        norm = split3(plane_sum(planes[:3], planes[:3]))
        closing = split3(plane_sum(planes[:3], planes[3:]))
        return split, norm, closing

    one = jnp.ones((chunks, 128), F32)
    zero = jnp.zeros((chunks, 128), F32)

    def put(which, row, value):
        feat[which, :, row, :] = value

    def prepare_source(block, planes, weights, parts):
        split, norm, closing = parts
        order = (0, 0, 0, 1, 1, 2)
        for n, piece in enumerate(order):
            for c in range(6):
                put(0, 18 * (c // 3) + 3 * n + c % 3, split[c][piece])
        for n in range(3):
            put(0, 36 + n, norm[n])
            put(0, 39 + n, closing[n])
            put(0, 42 + n, one)
            put(0, 45 + n, zero)
        for s in range(chunks):
            lhs[block, s * 128 : (s + 1) * 128, :] = feat[0, s].T.astype(BF16)
        heavy = [split3(weights * c) for c in planes] + [split3(weights)]
        for c in range(7):
            for n in range(3):
                put(1, 3 * c + n, heavy[c][n])
        for row in range(21, SUM_ROWS):
            put(1, row, zero)
        for s in range(chunks):
            weigh[block, :, s * 128 : (s + 1) * 128] = feat[1, s, 0:SUM_ROWS, :].astype(
                BF16
            )

    def prepare_target(parts):
        split, norm, closing = parts
        order = (0, 1, 2, 0, 1, 0)
        soft = split3(norm[0] + norm[1] + norm[2] + soften_sq)
        for n, piece in enumerate(order):
            for c in range(3):
                put(2, 3 * n + c, -2.0 * split[c][piece])
                put(2, 18 + 3 * n + c, zero)
                put(3, 3 * n + c, -split[3 + c][piece])
                put(3, 18 + 3 * n + c, -split[c][piece])
        for n in range(3):
            put(2, 36 + n, one)
            put(2, 39 + n, zero)
            put(2, 42 + n, soft[n])
            put(2, 45 + n, zero)
            put(3, 36 + n, zero)
            put(3, 39 + n, one)
            put(3, 42 + n, closing[n])
            put(3, 45 + n, zero)
        for s in range(chunks):
            rhs_r[:, s * 128 : (s + 1) * 128] = feat[2, s].astype(BF16)
            rhs_c[:, s * 128 : (s + 1) * 128] = feat[3, s].astype(BF16)

    def visit(block, first, begin=0, end=None):
        rows = lhs[block]
        weights = weigh[block]
        for n in range(chunks // wide)[begin:end]:
            cols = slice(n * wide * 128, (n + 1) * wide * 128)
            dist = jnp.dot(rows, rhs_r[:, cols], preferred_element_type=F32)
            closing = jnp.dot(rows, rhs_c[:, cols], preferred_element_type=F32)
            inverse = lax.rsqrt(dist)
            square = inverse * inverse
            strength = square * inverse
            turning = (closing * square) * strength
            s_high = strength.astype(BF16)
            s_low = (strength - s_high.astype(F32)).astype(BF16)
            t_high = turning.astype(BF16)
            new_s = jnp.dot(
                weights, s_high, preferred_element_type=F32
            ) + jnp.dot(weights, s_low, preferred_element_type=F32)
            new_t = jnp.dot(weights, t_high, preferred_element_type=F32)
            for m in range(wide):
                piece = slice(m * 128, (m + 1) * 128)
                if first:
                    sum_s[n * wide + m] = new_s[:, piece]
                    sum_t[n * wide + m] = new_t[:, piece]
                else:
                    sum_s[n * wide + m] += new_s[:, piece]
                    sum_t[n * wide + m] += new_t[:, piece]

    def forces(turn, planes, weights, src):
        parts = pieces(planes)
        prepare_source(0, planes, weights, parts)
        prepare_target(parts)
        if turn > 0:
            for k in range(1, nb):
                body_copy(turn, k, src).start()
        early = (chunks // wide) // 2
        if turn == 0:
            visit(0, True, 0, early)
            pl.semaphore_wait(barrier, (nb - 1) + (g - 1) + (ng - 1))
            for k in range(1, nb):
                body_copy(turn, k, src).start()
                mass_copy(k).start()
            visit(0, True, early)
        else:
            visit(0, True)
        for k in range(1, nb):
            body_copy(turn, k, src).wait_recv()
            if turn == 0:
                mass_copy(k).wait_recv()
            other = load_planes(got.at[turn, k - 1])
            prepare_source(k, other, got_mass[k - 1] * mass_scale, pieces(other))
            visit(k, False)

        def summed(ref, c):
            return ref[:, 3 * c, :] + ref[:, 3 * c + 1, :] + ref[:, 3 * c + 2, :]

        places, speeds = planes[:3], planes[3:]
        total, turned = summed(sum_s, 6), summed(sum_t, 6)
        inverse = lax.rsqrt(plane_sum(places, places))
        cube = inverse * inverse * inverse
        pull = 3.0 * plane_sum(places, speeds) * inverse * inverse
        acc, jerk = [], []
        for c in range(3):
            p, v = places[c], speeds[c]
            acc.append(summed(sum_s, c) - p * total - cube * p)
            spin = summed(sum_s, 3 + c) - v * total
            spin = spin - 3.0 * (summed(sum_t, c) - p * turned)
            jerk.append(spin - cube * (v - pull * p))
        return acc, jerk

    for copy in arrivals:
        copy.wait()
    planes = load_planes(state_ref)
    weights = mass_ref[...] * mass_scale
    h = fine_step
    acc, jerk = forces(0, planes, weights, state_ref)
    for step in range(2):
        pos, vel = planes[:3], planes[3:]
        guess = tuple(
            p + h * v + h * h / 2.0 * a + h**3 / 6.0 * j
            for p, v, a, j in zip(pos, vel, acc, jerk)
        ) + tuple(v + h * a + h * h / 2.0 * j for v, a, j in zip(vel, acc, jerk))
        out = sendbuf.at[step]
        store_planes(out, guess)
        na, nj = forces(step + 1, guess, weights, out)
        new_vel = tuple(
            vel[c] + h / 2.0 * (acc[c] + na[c]) + h * h / 12.0 * (jerk[c] - nj[c])
            for c in range(3)
        )
        new_pos = tuple(
            pos[c] + h / 2.0 * (vel[c] + new_vel[c]) + h * h / 12.0 * (acc[c] - na[c])
            for c in range(3)
        )
        planes, acc, jerk = new_pos + new_vel, na, nj

    freq = freq_ref[...]
    angle = freq * slice_time
    cos1, sin1 = jnp.cos(angle), jnp.sin(angle)
    fine = planes
    own = load_planes(state_ref)
    coarse = drift(own, cos1, sin1, freq)
    corr = tuple(a - b for a, b in zip(fine, coarse))
    first = slot == 0
    store_planes(grp.at[r], tuple(jnp.where(first, a, b) for a, b in zip(fine, corr)))
    store_planes(fine_ref, fine)
    store_planes(corr_ref, corr)

    def grp_copy(k):
        return pltpu.make_async_remote_copy(
            src_ref=grp.at[r], dst_ref=grp.at[r],
            send_sem=grp_send.at[k - 1], recv_sem=grp_recv.at[r],
            device_id={"tm": q * g + (r + k) % g},
        )

    def grp_arrival(k):
        source = (r + g - k) % g
        return pltpu.make_async_remote_copy(
            src_ref=grp.at[source], dst_ref=grp.at[source],
            send_sem=grp_send.at[k - 1], recv_sem=grp_recv.at[source],
            device_id={"tm": q * g + (r + k) % g},
        )

    for k in range(1, g):
        grp_copy(k).start()
    leaving = [
        pltpu.make_async_copy(src, out_hbm.at[n], out_sem.at[n])
        for n, src in enumerate((fine_ref, corr_ref, next_ref))
    ]
    leaving[0].start()
    leaving[1].start()
    angle_g = float(g) * freq * slice_time
    cosg, sing = jnp.cos(angle_g), jnp.sin(angle_g)
    for k in range(1, g):
        grp_arrival(k).wait_recv()

    def tot_copy(k):
        return pltpu.make_async_remote_copy(
            src_ref=tot, dst_ref=carry_in.at[k - 1],
            send_sem=tot_send.at[k - 1], recv_sem=tot_recv.at[k - 1],
            device_id={"tm": ((q + k) % ng) * g + r},
        )

    if ng > 1:
        value = load_planes(grp.at[0])
        for m in range(1, g):
            moved = drift(value, cos1, sin1, freq)
            value = tuple(a + b for a, b in zip(moved, load_planes(grp.at[m])))
        store_planes(tot, value)
        for k in range(1, ng):
            @pl.when(q + k < ng)
            def _(k=k):
                tot_copy(k).start()

    value = tuple(jnp.zeros_like(freq) for _ in range(6))
    for k in range(ng - 1, 0, -1):
        @pl.when(k <= q)
        def _(k=k):
            tot_copy(k).wait_recv()

        here = k <= q
        moved = drift(value, cosg, sing, freq)
        value = tuple(
            jnp.where(here, a + b, c)
            for a, b, c in zip(moved, load_planes(carry_in.at[k - 1]), value)
        )
    for m in range(g - 1):
        here = m < r
        moved = drift(value, cos1, sin1, freq)
        value = tuple(
            jnp.where(here, a + b, c)
            for a, b, c in zip(moved, load_planes(grp.at[m]), value)
        )
    store_planes(next_ref, tuple(jnp.where(first, a, b) for a, b in zip(own, value)))

    leaving[2].start()
    for k in range(1, nb):
        body_copy(0, k, state_ref).wait_send()
        mass_copy(k).wait_send()
        for step in range(2):
            body_copy(step + 1, k, sendbuf.at[step]).wait_send()
    for k in range(1, g):
        grp_copy(k).wait_send()
    for k in range(1, ng):
        @pl.when(q + k < ng)
        def _(k=k):
            tot_copy(k).wait_send()
    for copy in leaving:
        copy.wait()


def solution(mesh):
    nt = mesh.shape["tm"]
    nb = mesh.shape["body"]
    g = group_size(nt)
    ng = nt // g

    def local(states, masses, frequency):
        lanes = states.shape[2]
        s = lanes // 128
        dma = pltpu.SemaphoreType.DMA
        anywhere = pl.BlockSpec(memory_space=pl.ANY)
        outs = pl.pallas_call(
            functools.partial(kernel, nt, nb, g),
            out_shape=jax.ShapeDtypeStruct((3, 6, s, 128), F32),
            in_specs=[anywhere] * 3,
            out_specs=anywhere,
            scratch_shapes=[
                pltpu.VMEM((6, s, 128), F32),
                pltpu.VMEM((s, 128), F32),
                pltpu.VMEM((s, 128), F32),
                pltpu.VMEM((6, s, 128), F32),
                pltpu.VMEM((6, s, 128), F32),
                pltpu.VMEM((6, s, 128), F32),
                pltpu.VMEM((4, s, FEATURES, 128), F32),
                pltpu.VMEM((nb, lanes, FEATURES), BF16),
                pltpu.VMEM((nb, SUM_ROWS, lanes), BF16),
                pltpu.VMEM((FEATURES, lanes), BF16),
                pltpu.VMEM((FEATURES, lanes), BF16),
                pltpu.VMEM((s, SUM_ROWS, 128), F32),
                pltpu.VMEM((s, SUM_ROWS, 128), F32),
                pltpu.VMEM((2, 6, s, 128), F32),
                pltpu.VMEM((3, max(nb - 1, 1), 6, s, 128), F32),
                pltpu.VMEM((max(nb - 1, 1), s, 128), F32),
                pltpu.VMEM((g, 6, s, 128), F32),
                pltpu.VMEM((6, s, 128), F32),
                pltpu.VMEM((max(ng - 1, 1), 6, s, 128), F32),
                dma((3,)),
                dma((3,)),
                dma((3, max(nb - 1, 1))),
                dma((3, max(nb - 1, 1))),
                dma((max(nb - 1, 1),)),
                dma((max(nb - 1, 1),)),
                dma((max(g - 1, 1),)),
                dma((g,)),
                dma((max(ng - 1, 1),)),
                dma((max(ng - 1, 1),)),
            ],
            compiler_params=pltpu.CompilerParams(
                collective_id=0, has_side_effects=True
            ),
        )(
            states.reshape(6, s, 128),
            masses.reshape(s, 128),
            frequency.reshape(s, 128),
        )
        return tuple(outs[n].reshape(1, 6, lanes) for n in range(3))

    placed = (P("tm", None, "body"), P("body"), P("body"))
    return jax.shard_map(
        local,
        mesh=mesh,
        in_specs=placed,
        out_specs=(P("tm", None, "body"),) * 3,
        check_vma=False,
    )
```

profile of v0, /device:TPU:24, one launch (start us, length us, event | category | flops | bytes accessed | tf_op | source)
XLA Modules:
  0.0 27.3 jit_solution(7465110729873599132)
XLA Ops:
  0.6 25.2 %shard_map.58 = f32[3,6,8,128]{3,2,1,0:T(8,128)} custom-call(f32[6,8,128]{2,1,0:T(8,128)} %bitcast.9, f32[8,128]{1,0:T(8,128)} %bitcast.10, f32[8,128]{1,0:T(8,128)} %bitcast.11), custom_call_target="tpu_custom_call" | custom-call | tf_op jit(solution)/shard_map/pallas_call | solution.py:372
  25.9 1.4 %fusion = (f32[1,6,8,128]{3,2,1,0:T(8,128)}, f32[1,6,8,128]{3,2,1,0:T(8,128)}, f32[1,6,8,128]{3,2,1,0:T(8,128)}) fusion(f32[3,6,8,128]{3,2,1,0:T(8,128)} %shard_map.58), kind=kLoop, calls=%fused_computation | loop fusion | bytes 147456 | tf_op jit(solution)/shard_map/slice | solution.py:416
where the time goes:
time: 27.8 us; the launch traced here: 27.3 us
  Pallas kernels  25.2 us (91%)
  local copies, waits for them, and re-layouts  1.4 us (5%)
  between operations  0.64 us (2%)
    pallas_call x1, Pallas kernels, local(): pl.pallas_call(functools.partial(kernel, nt, nb, g), out_shape=jax.ShapeD...  25.2 us
    slice x1, local copies, waits for them, and re-layouts, local(): return tuple((outs[n].reshape(1, 6, lanes) for n in range(3)))  1.4 us

commit v1 on v0

--- a/solution.py
+++ b/solution.py
@@ -15,7 +15,8 @@
 F32 = jnp.float32
 BF16 = jnp.bfloat16
 FEATURES = 48
-SUM_ROWS = 32
+SUM_ROWS = 16
+HALF_ROWS = 8
 TILE_I = 256
 
 
@@ -32,6 +33,11 @@
     rest = value - high
     middle = rest.astype(BF16).astype(F32)
     return high, middle, rest - middle
+
+
+def split2(value):
+    high = value.astype(BF16).astype(F32)
+    return high, value - high
 
 
 def drift(planes, cos_turn, sin_turn, frequency):
@@ -68,7 +74,7 @@
     sendbuf, got, got_mass, grp, tot, carry_in,
     in_sem, out_sem,
     body_send, body_recv, mass_send, mass_recv,
-    grp_send, grp_recv, tot_send, tot_recv,
+    grp_send, grp_recv, tot_send, tot_recv, entered,
 ):
     slot = lax.axis_index("tm")
     half = lax.axis_index("body")
@@ -78,15 +84,58 @@
     chunks = state_ref.shape[1]
     lanes = chunks * 128
     wide = TILE_I // 128 if chunks % (TILE_I // 128) == 0 else 1
+    span = wide * 128
+    touched = set()
     mass_scale = disc_mass / (lanes * nb)
 
     barrier = pltpu.get_barrier_semaphore()
-    for k in range(1, nb):
-        pl.semaphore_signal(barrier, inc=1, device_id={"body": (half + k) % nb})
-    for k in range(1, g):
-        pl.semaphore_signal(barrier, inc=1, device_id={"tm": q * g + (r + k) % g})
-    for k in range(1, ng):
-        pl.semaphore_signal(barrier, inc=1, device_id={"tm": ((q + k) % ng) * g + r})
+    split = nb == 2
+    later_peers = (g - 1) + (ng - 1)
+
+    def greet_slices():
+        for k in range(1, g):
+            pl.semaphore_signal(barrier, inc=1, device_id={"tm": q * g + (r + k) % g})
+        for k in range(1, ng):
+            pl.semaphore_signal(
+                barrier, inc=1, device_id={"tm": ((q + k) % ng) * g + r}
+            )
+
+    def greet():
+        if split:
+            @pl.when(half == 1)
+            def _():
+                pl.semaphore_signal(barrier, inc=1, device_id={"body": 1 - half})
+        else:
+            for k in range(1, nb):
+                pl.semaphore_signal(barrier, inc=1, device_id={"body": (half + k) % nb})
+            greet_slices()
+
+    def meet_partner():
+        if split:
+            @pl.when(half == 0)
+            def _():
+                pl.semaphore_wait(barrier, 1)
+                pl.semaphore_signal(entered.at[0], inc=1, device_id={"body": 1 - half})
+
+            @pl.when(half == 1)
+            def _():
+                pl.semaphore_wait(entered.at[0], 1)
+                greet_slices()
+        else:
+            pl.semaphore_wait(barrier, (nb - 1) + later_peers)
+
+    def meet_slices():
+        if split and later_peers:
+            @pl.when(half == 1)
+            def _():
+                pl.semaphore_wait(barrier, later_peers)
+                pl.semaphore_signal(entered.at[1], inc=1, device_id={"body": 1 - half})
+
+            @pl.when(half == 0)
+            def _():
+                pl.semaphore_wait(entered.at[1], 1)
+
+    greet()
     arrivals = [
         pltpu.make_async_copy(src, dst, in_sem.at[n])
         for n, (src, dst) in enumerate(
@@ -121,6 +170,21 @@
 
     def put(which, row, value):
         feat[which, :, row, :] = value
+
+    def prepare_constants():
+        for row in range(18):
+            put(2, 18 + row, zero)
+        for n in range(3):
+            put(0, 42 + n, one)
+            put(0, 45 + n, zero)
+            put(2, 36 + n, one)
+            put(2, 39 + n, zero)
+            put(2, 45 + n, zero)
+            put(3, 36 + n, zero)
+            put(3, 39 + n, one)
+            put(3, 45 + n, zero)
+        for n in range(2):
+            put(1, HALF_ROWS * n + 7, zero)
 
     def prepare_source(block, planes, weights, parts):
         split, norm, closing = parts
@@ -131,16 +195,12 @@
         for n in range(3):
             put(0, 36 + n, norm[n])
             put(0, 39 + n, closing[n])
-            put(0, 42 + n, one)
-            put(0, 45 + n, zero)
         for s in range(chunks):
             lhs[block, s * 128 : (s + 1) * 128, :] = feat[0, s].T.astype(BF16)
-        heavy = [split3(weights * c) for c in planes] + [split3(weights)]
+        heavy = [split2(weights * c) for c in planes] + [split2(weights)]
         for c in range(7):
-            for n in range(3):
-                put(1, 3 * c + n, heavy[c][n])
-        for row in range(21, SUM_ROWS):
-            put(1, row, zero)
+            for n in range(2):
+                put(1, HALF_ROWS * n + c, heavy[c][n])
         for s in range(chunks):
             weigh[block, :, s * 128 : (s + 1) * 128] = feat[1, s, 0:SUM_ROWS, :].astype(
                 BF16
@@ -153,48 +213,68 @@
         for n, piece in enumerate(order):
             for c in range(3):
                 put(2, 3 * n + c, -2.0 * split[c][piece])
-                put(2, 18 + 3 * n + c, zero)
                 put(3, 3 * n + c, -split[3 + c][piece])
                 put(3, 18 + 3 * n + c, -split[c][piece])
         for n in range(3):
-            put(2, 36 + n, one)
-            put(2, 39 + n, zero)
             put(2, 42 + n, soft[n])
-            put(2, 45 + n, zero)
-            put(3, 36 + n, zero)
-            put(3, 39 + n, one)
             put(3, 42 + n, closing[n])
-            put(3, 45 + n, zero)
         for s in range(chunks):
             rhs_r[:, s * 128 : (s + 1) * 128] = feat[2, s].astype(BF16)
             rhs_c[:, s * 128 : (s + 1) * 128] = feat[3, s].astype(BF16)
 
-    def visit(block, first, begin=0, end=None):
-        rows = lhs[block]
-        weights = weigh[block]
-        for n in range(chunks // wide)[begin:end]:
-            cols = slice(n * wide * 128, (n + 1) * wide * 128)
+    def visit(tiles):
+        def pair(tile):
+            block, at, n = tile
+            rows = lhs[block, at * span : (at + 1) * span, :]
+            cols = slice(n * span, (n + 1) * span)
             dist = jnp.dot(rows, rhs_r[:, cols], preferred_element_type=F32)
             closing = jnp.dot(rows, rhs_c[:, cols], preferred_element_type=F32)
+            return dist, closing
+
+        def curve(dist, closing):
             inverse = lax.rsqrt(dist)
             square = inverse * inverse
             strength = square * inverse
             turning = (closing * square) * strength
             s_high = strength.astype(BF16)
             s_low = (strength - s_high.astype(F32)).astype(BF16)
-            t_high = turning.astype(BF16)
-            new_s = jnp.dot(
-                weights, s_high, preferred_element_type=F32
-            ) + jnp.dot(weights, s_low, preferred_element_type=F32)
-            new_t = jnp.dot(weights, t_high, preferred_element_type=F32)
+            return s_high, s_low, turning.astype(BF16)
+
+        def collect(block, at, n, parts, dims):
+            weights = weigh[block, :, at * span : (at + 1) * span]
+            new = [
+                lax.dot_general(weights, part, (dims, ((), ())), preferred_element_type=F32)
+                for part in parts
+            ]
+            new_s, new_t = (
+                a[:HALF_ROWS] + a[HALF_ROWS:] for a in (new[0] + new[1], new[2])
+            )
+            fresh = n not in touched
+            touched.add(n)
             for m in range(wide):
                 piece = slice(m * 128, (m + 1) * 128)
-                if first:
+                if fresh:
                     sum_s[n * wide + m] = new_s[:, piece]
                     sum_t[n * wide + m] = new_t[:, piece]
                 else:
                     sum_s[n * wide + m] += new_s[:, piece]
                     sum_t[n * wide + m] += new_t[:, piece]
+
+        def gather(tile, parts):
+            block, at, n = tile
+            collect(block, at, n, parts, ((1,), (0,)))
+            if block == 0 and at != n:
+                collect(block, n, at, parts, ((1,), (1,)))
+
+        ready, parts = pair(tiles[0]), None
+        for index in range(len(tiles)):
+            now = ready
+            if index + 1 < len(tiles):
+                ready = pair(tiles[index + 1])
+            if index > 0:
+                gather(tiles[index - 1], parts)
+            parts = curve(*now)
+        gather(tiles[-1], parts)
 
     def forces(turn, planes, weights, src):
         parts = pieces(planes)
@@ -203,26 +283,30 @@
         if turn > 0:
             for k in range(1, nb):
                 body_copy(turn, k, src).start()
-        early = (chunks // wide) // 2
+        touched.clear()
+        squares = range(chunks // wide)
+        own = [(0, at, n) for n in squares for at in squares if at >= n]
+        early = 0 if split else (len(own) + 1) // 2
         if turn == 0:
-            visit(0, True, 0, early)
-            pl.semaphore_wait(barrier, (nb - 1) + (g - 1) + (ng - 1))
+            if early:
+                visit(own[:early])
+            meet_partner()
             for k in range(1, nb):
                 body_copy(turn, k, src).start()
                 mass_copy(k).start()
-            visit(0, True, early)
+            visit(own[early:])
         else:
-            visit(0, True)
+            visit(own)
         for k in range(1, nb):
             body_copy(turn, k, src).wait_recv()
             if turn == 0:
                 mass_copy(k).wait_recv()
             other = load_planes(got.at[turn, k - 1])
             prepare_source(k, other, got_mass[k - 1] * mass_scale, pieces(other))
-            visit(k, False)
+            visit([(k, at, n) for n in squares for at in squares])
 
         def summed(ref, c):
-            return ref[:, 3 * c, :] + ref[:, 3 * c + 1, :] + ref[:, 3 * c + 2, :]
+            return ref[:, c, :]
 
         places, speeds = planes[:3], planes[3:]
         total, turned = summed(sum_s, 6), summed(sum_t, 6)
@@ -238,6 +322,7 @@
             jerk.append(spin - cube * (v - pull * p))
         return acc, jerk
 
+    prepare_constants()
     for copy in arrivals:
         copy.wait()
     planes = load_planes(state_ref)
@@ -262,6 +347,8 @@
             for c in range(3)
         )
         planes, acc, jerk = new_pos + new_vel, na, nj
+        if step == 0:
+            meet_slices()
 
     freq = freq_ref[...]
     angle = freq * slice_time
@@ -386,8 +473,8 @@
                 pltpu.VMEM((nb, SUM_ROWS, lanes), BF16),
                 pltpu.VMEM((FEATURES, lanes), BF16),
                 pltpu.VMEM((FEATURES, lanes), BF16),
-                pltpu.VMEM((s, SUM_ROWS, 128), F32),
-                pltpu.VMEM((s, SUM_ROWS, 128), F32),
+                pltpu.VMEM((s, HALF_ROWS, 128), F32),
+                pltpu.VMEM((s, HALF_ROWS, 128), F32),
                 pltpu.VMEM((2, 6, s, 128), F32),
                 pltpu.VMEM((3, max(nb - 1, 1), 6, s, 128), F32),
                 pltpu.VMEM((max(nb - 1, 1), s, 128), F32),
@@ -404,6 +491,7 @@
                 dma((g,)),
                 dma((max(ng - 1, 1),)),
                 dma((max(ng - 1, 1),)),
+                pltpu.SemaphoreType.REGULAR((2,)),
             ],
             compiler_params=pltpu.CompilerParams(
                 collective_id=0, has_side_effects=True

time: 27.8 us -> 24.5 us (0.88); the launches traced: 27.3 us -> 24.3 us
  Pallas kernels: 25.2 us -> 22.2 us
    pallas_call x1, Pallas kernels: 25.2 us -> 22.2 us  [local(): pl.pallas_call(functools.partial(kernel, nt, nb, g), out_shape=jax.ShapeD...]
where the time goes in v1:
time: 24.5 us; the launch traced here: 24.3 us
  Pallas kernels  22.2 us (91%)
  local copies, waits for them, and re-layouts  1.4 us (6%)
  between operations  0.64 us (3%)
    pallas_call x1, Pallas kernels, local(): pl.pallas_call(functools.partial(kernel, nt, nb, g), out_shape=jax.ShapeD...  22.2 us
    slice x1, local copies, waits for them, and re-layouts, local(): return tuple((outs[n].reshape(1, 6, lanes) for n in range(3)))  1.4 us

profile of v1, /device:TPU:24, one launch (start us, length us, event | category | flops | bytes accessed | tf_op | source)
XLA Modules:
  0.0 24.3 jit_solution(9618444607768979507)
XLA Ops:
  0.6 22.2 %shard_map.58 = f32[3,6,8,128]{3,2,1,0:T(8,128)} custom-call(f32[6,8,128]{2,1,0:T(8,128)} %bitcast.9, f32[8,128]{1,0:T(8,128)} %bitcast.10, f32[8,128]{1,0:T(8,128)} %bitcast.11), custom_call_target="tpu_custom_call" | custom-call | tf_op jit(solution)/shard_map/pallas_call | solution.py:459
  22.9 1.4 %fusion = (f32[1,6,8,128]{3,2,1,0:T(8,128)}, f32[1,6,8,128]{3,2,1,0:T(8,128)}, f32[1,6,8,128]{3,2,1,0:T(8,128)}) fusion(f32[3,6,8,128]{3,2,1,0:T(8,128)} %shard_map.58), kind=kLoop, calls=%fused_computation | loop fusion | bytes 147456 | tf_op jit(solution)/shard_map/slice | solution.py:504

commit v2 on v1

--- a/solution.py
+++ b/solution.py
@@ -68,11 +68,11 @@
 def kernel(
     nt, nb, g,
     state_hbm, mass_hbm, freq_hbm,
-    out_hbm,
-    state_ref, mass_ref, freq_ref, fine_ref, corr_ref, next_ref,
-    feat, lhs, weigh, rhs_r, rhs_c, sum_s, sum_t,
-    sendbuf, got, got_mass, grp, tot, carry_in,
-    in_sem, out_sem,
+    out_ref,
+    state_ref, mass_ref, freq_ref,
+    lhs, weigh, rhs_r, rhs_c, sum_s, sum_t,
+    rows, got, got_mass, grp, tot, carry_in,
+    in_sem,
     body_send, body_recv, mass_send, mass_recv,
     grp_send, grp_recv, tot_send, tot_recv, entered,
 ):
@@ -145,9 +145,9 @@
     for copy in arrivals:
         copy.start()
 
-    def body_copy(turn, k, src):
+    def body_copy(turn, k):
         return pltpu.make_async_remote_copy(
-            src_ref=src, dst_ref=got.at[turn, k - 1],
+            src_ref=rows.at[turn], dst_ref=got.at[turn, k - 1],
             send_sem=body_send.at[turn, k - 1], recv_sem=body_recv.at[turn, k - 1],
             device_id={"body": (half + k) % nb},
         )
@@ -159,68 +159,50 @@
             device_id={"body": (half + k) % nb},
         )
 
-    def pieces(planes):
-        split = [split3(c) for c in planes]
-        norm = split3(plane_sum(planes[:3], planes[:3]))
-        closing = split3(plane_sum(planes[:3], planes[3:]))
-        return split, norm, closing
-
-    one = jnp.ones((chunks, 128), F32)
-    zero = jnp.zeros((chunks, 128), F32)
-
-    def put(which, row, value):
-        feat[which, :, row, :] = value
-
-    def prepare_constants():
-        for row in range(18):
-            put(2, 18 + row, zero)
-        for n in range(3):
-            put(0, 42 + n, one)
-            put(0, 45 + n, zero)
-            put(2, 36 + n, one)
-            put(2, 39 + n, zero)
-            put(2, 45 + n, zero)
-            put(3, 36 + n, zero)
-            put(3, 39 + n, one)
-            put(3, 45 + n, zero)
-        for n in range(2):
-            put(1, HALF_ROWS * n + 7, zero)
-
-    def prepare_source(block, planes, weights, parts):
-        split, norm, closing = parts
-        order = (0, 0, 0, 1, 1, 2)
-        for n, piece in enumerate(order):
-            for c in range(6):
-                put(0, 18 * (c // 3) + 3 * n + c % 3, split[c][piece])
-        for n in range(3):
-            put(0, 36 + n, norm[n])
-            put(0, 39 + n, closing[n])
+    row = lax.broadcasted_iota(jnp.int32, (8, 128), 0)
+    norm_row, closing_row = row == 3, row == 7
+    free_row = norm_row | closing_row
+    to_dist = jnp.where(row < 3, -2.0, jnp.where(norm_row, 1.0, 0.0))
+    soften = jnp.where(norm_row, soften_sq, 0.0)
+    to_closing = jnp.where(norm_row, 1.0, jnp.where(closing_row, 0.0, -1.0))
+
+    def publish(turn, planes):
+        places, speeds = planes[:3], planes[3:]
+        order = places + (plane_sum(places, places),)
+        order = order + speeds + (plane_sum(places, speeds),)
+        for c in range(8):
+            rows[turn, :, c, :] = order[c]
+
+    def prepare_source(block, ref, mass):
         for s in range(chunks):
-            lhs[block, s * 128 : (s + 1) * 128, :] = feat[0, s].T.astype(BF16)
-        heavy = [split2(weights * c) for c in planes] + [split2(weights)]
-        for c in range(7):
-            for n in range(2):
-                put(1, HALF_ROWS * n + c, heavy[c][n])
+            body = ref[s]
+            high, middle, low = split3(body)
+            first = jnp.where(free_row, 1.0, high)
+            second = jnp.where(free_row, 1.0, middle)
+            feature = jnp.concatenate([high, first, first, middle, second, low], axis=0)
+            lhs[block, s * 128 : (s + 1) * 128, :] = feature.astype(BF16).T
+            weight = jnp.broadcast_to(mass[s : s + 1, :], (8, 128)) * mass_scale
+            heavy = jnp.where(closing_row, 0.0, weight * body)
+            heavy = split2(jnp.where(norm_row, weight, heavy))
+            weigh[block, :, s * 128 : (s + 1) * 128] = jnp.concatenate(
+                heavy, axis=0
+            ).astype(BF16)
+
+    def prepare_target(ref):
         for s in range(chunks):
-            weigh[block, :, s * 128 : (s + 1) * 128] = feat[1, s, 0:SUM_ROWS, :].astype(
-                BF16
-            )
-
-    def prepare_target(parts):
-        split, norm, closing = parts
-        order = (0, 1, 2, 0, 1, 0)
-        soft = split3(norm[0] + norm[1] + norm[2] + soften_sq)
-        for n, piece in enumerate(order):
-            for c in range(3):
-                put(2, 3 * n + c, -2.0 * split[c][piece])
-                put(3, 3 * n + c, -split[3 + c][piece])
-                put(3, 18 + 3 * n + c, -split[c][piece])
-        for n in range(3):
-            put(2, 42 + n, soft[n])
-            put(3, 42 + n, closing[n])
-        for s in range(chunks):
-            rhs_r[:, s * 128 : (s + 1) * 128] = feat[2, s].astype(BF16)
-            rhs_c[:, s * 128 : (s + 1) * 128] = feat[3, s].astype(BF16)
+            body = ref[s]
+            high, middle, low = split3(to_dist * body + soften)
+            one = jnp.where(norm_row, 1.0, high)
+            cross = jnp.where(norm_row, high, middle)
+            rhs_r[:, s * 128 : (s + 1) * 128] = jnp.concatenate(
+                [one, middle, low, one, cross, one], axis=0
+            ).astype(BF16)
+            high, middle, low = split3(to_closing * pltpu.roll(body, 4, 0))
+            one = jnp.where(free_row, jnp.where(norm_row, 0.0, 1.0), high)
+            cross = jnp.where(norm_row, high, middle)
+            rhs_c[:, s * 128 : (s + 1) * 128] = jnp.concatenate(
+                [one, middle, low, one, cross, one], axis=0
+            ).astype(BF16)
 
     def visit(tiles):
         def pair(tile):
@@ -276,40 +258,31 @@
             parts = curve(*now)
         gather(tiles[-1], parts)
 
-    def forces(turn, planes, weights, src):
-        parts = pieces(planes)
-        prepare_source(0, planes, weights, parts)
-        prepare_target(parts)
-        if turn > 0:
-            for k in range(1, nb):
-                body_copy(turn, k, src).start()
+    def forces(turn, planes):
+        publish(turn, planes)
+        if turn == 0:
+            meet_partner()
+        for k in range(1, nb):
+            body_copy(turn, k).start()
+            if turn == 0:
+                mass_copy(k).start()
+        prepare_source(0, rows.at[turn], mass_ref)
+        prepare_target(rows.at[turn])
         touched.clear()
         squares = range(chunks // wide)
-        own = [(0, at, n) for n in squares for at in squares if at >= n]
-        early = 0 if split else (len(own) + 1) // 2
-        if turn == 0:
-            if early:
-                visit(own[:early])
-            meet_partner()
-            for k in range(1, nb):
-                body_copy(turn, k, src).start()
-                mass_copy(k).start()
-            visit(own[early:])
-        else:
-            visit(own)
+        visit([(0, at, n) for n in squares for at in squares if at >= n])
         for k in range(1, nb):
-            body_copy(turn, k, src).wait_recv()
+            body_copy(turn, k).wait_recv()
             if turn == 0:
                 mass_copy(k).wait_recv()
-            other = load_planes(got.at[turn, k - 1])
-            prepare_source(k, other, got_mass[k - 1] * mass_scale, pieces(other))
+            prepare_source(k, got.at[turn, k - 1], got_mass.at[k - 1])
             visit([(k, at, n) for n in squares for at in squares])
 
         def summed(ref, c):
             return ref[:, c, :]
 
         places, speeds = planes[:3], planes[3:]
-        total, turned = summed(sum_s, 6), summed(sum_t, 6)
+        total, turned = summed(sum_s, 3), summed(sum_t, 3)
         inverse = lax.rsqrt(plane_sum(places, places))
         cube = inverse * inverse * inverse
         pull = 3.0 * plane_sum(places, speeds) * inverse * inverse
@@ -317,27 +290,23 @@
         for c in range(3):
             p, v = places[c], speeds[c]
             acc.append(summed(sum_s, c) - p * total - cube * p)
-            spin = summed(sum_s, 3 + c) - v * total
+            spin = summed(sum_s, 4 + c) - v * total
             spin = spin - 3.0 * (summed(sum_t, c) - p * turned)
             jerk.append(spin - cube * (v - pull * p))
         return acc, jerk
 
-    prepare_constants()
     for copy in arrivals:
         copy.wait()
     planes = load_planes(state_ref)
-    weights = mass_ref[...] * mass_scale
     h = fine_step
-    acc, jerk = forces(0, planes, weights, state_ref)
+    acc, jerk = forces(0, planes)
     for step in range(2):
         pos, vel = planes[:3], planes[3:]
         guess = tuple(
             p + h * v + h * h / 2.0 * a + h**3 / 6.0 * j
             for p, v, a, j in zip(pos, vel, acc, jerk)
         ) + tuple(v + h * a + h * h / 2.0 * j for v, a, j in zip(vel, acc, jerk))
-        out = sendbuf.at[step]
-        store_planes(out, guess)
-        na, nj = forces(step + 1, guess, weights, out)
+        na, nj = forces(step + 1, guess)
         new_vel = tuple(
             vel[c] + h / 2.0 * (acc[c] + na[c]) + h * h / 12.0 * (jerk[c] - nj[c])
             for c in range(3)
@@ -359,8 +328,8 @@
     corr = tuple(a - b for a, b in zip(fine, coarse))
     first = slot == 0
     store_planes(grp.at[r], tuple(jnp.where(first, a, b) for a, b in zip(fine, corr)))
-    store_planes(fine_ref, fine)
-    store_planes(corr_ref, corr)
+    store_planes(out_ref.at[0], fine)
+    store_planes(out_ref.at[1], corr)
 
     def grp_copy(k):
         return pltpu.make_async_remote_copy(
@@ -379,12 +348,6 @@
 
     for k in range(1, g):
         grp_copy(k).start()
-    leaving = [
-        pltpu.make_async_copy(src, out_hbm.at[n], out_sem.at[n])
-        for n, src in enumerate((fine_ref, corr_ref, next_ref))
-    ]
-    leaving[0].start()
-    leaving[1].start()
     angle_g = float(g) * freq * slice_time
     cosg, sing = jnp.cos(angle_g), jnp.sin(angle_g)
     for k in range(1, g):
@@ -427,22 +390,18 @@
             jnp.where(here, a + b, c)
             for a, b, c in zip(moved, load_planes(grp.at[m]), value)
         )
-    store_planes(next_ref, tuple(jnp.where(first, a, b) for a, b in zip(own, value)))
-
-    leaving[2].start()
+    store_planes(out_ref.at[2], tuple(jnp.where(first, a, b) for a, b in zip(own, value)))
+
     for k in range(1, nb):
-        body_copy(0, k, state_ref).wait_send()
         mass_copy(k).wait_send()
-        for step in range(2):
-            body_copy(step + 1, k, sendbuf.at[step]).wait_send()
+        for turn in range(3):
+            body_copy(turn, k).wait_send()
     for k in range(1, g):
         grp_copy(k).wait_send()
     for k in range(1, ng):
         @pl.when(q + k < ng)
         def _(k=k):
             tot_copy(k).wait_send()
-    for copy in leaving:
-        copy.wait()
 
 
 def solution(mesh):
@@ -458,30 +417,25 @@
         anywhere = pl.BlockSpec(memory_space=pl.ANY)
         outs = pl.pallas_call(
             functools.partial(kernel, nt, nb, g),
-            out_shape=jax.ShapeDtypeStruct((3, 6, s, 128), F32),
+            out_shape=pltpu.VMEM((3, 6, s, 128), F32),
             in_specs=[anywhere] * 3,
-            out_specs=anywhere,
+            out_specs=pl.BlockSpec(memory_space=pltpu.VMEM),
             scratch_shapes=[
                 pltpu.VMEM((6, s, 128), F32),
                 pltpu.VMEM((s, 128), F32),
                 pltpu.VMEM((s, 128), F32),
-                pltpu.VMEM((6, s, 128), F32),
-                pltpu.VMEM((6, s, 128), F32),
-                pltpu.VMEM((6, s, 128), F32),
-                pltpu.VMEM((4, s, FEATURES, 128), F32),
                 pltpu.VMEM((nb, lanes, FEATURES), BF16),
                 pltpu.VMEM((nb, SUM_ROWS, lanes), BF16),
                 pltpu.VMEM((FEATURES, lanes), BF16),
                 pltpu.VMEM((FEATURES, lanes), BF16),
                 pltpu.VMEM((s, HALF_ROWS, 128), F32),
                 pltpu.VMEM((s, HALF_ROWS, 128), F32),
-                pltpu.VMEM((2, 6, s, 128), F32),
-                pltpu.VMEM((3, max(nb - 1, 1), 6, s, 128), F32),
+                pltpu.VMEM((3, s, 8, 128), F32),
+                pltpu.VMEM((3, max(nb - 1, 1), s, 8, 128), F32),
                 pltpu.VMEM((max(nb - 1, 1), s, 128), F32),
                 pltpu.VMEM((g, 6, s, 128), F32),
                 pltpu.VMEM((6, s, 128), F32),
                 pltpu.VMEM((max(ng - 1, 1), 6, s, 128), F32),
-                dma((3,)),
                 dma((3,)),
                 dma((3, max(nb - 1, 1))),
                 dma((3, max(nb - 1, 1))),

time: 24.5 us -> 22.2 us (0.906)
  the two profiles are of different devices: /device:TPU:24 before, /device:TPU:0 now
where the time goes in v2:
time: 22.2 us; the launch traced here: 22 us
  Pallas kernels  20.7 us (93%)
  between operations  0.64 us (3%)
  local copies, waits for them, and re-layouts  0.63 us (3%)
    pallas_call x1, Pallas kernels, local(): pl.pallas_call(functools.partial(kernel, nt, nb, g), out_shape=pltpu.VMEM...  20.7 us
    slice x1, local copies, waits for them, and re-layouts, local(): return tuple((outs[n].reshape(1, 6, lanes) for n in range(3)))  0.63 us

profile of v2, /device:TPU:0, one launch (start us, length us, event | category | flops | bytes accessed | tf_op | source)
XLA Modules:
  0.0 22.0 jit_solution(5488819630051066390)
XLA Ops:
  0.6 20.7 %shard_map.58 = f32[3,6,8,128]{3,2,1,0:T(8,128)S(1)} custom-call(f32[6,8,128]{2,1,0:T(8,128)} %bitcast.9, f32[8,128]{1,0:T(8,128)} %bitcast.10, f32[8,128]{1,0:T(8,128)} %bitcast.11), custom_call_target="tpu_custom_call" | custom-call | tf_op jit(solution)/shard_map/pallas_call | solution.py:418
  21.4 0.6 %fusion = (f32[1,6,8,128]{3,2,1,0:T(8,128)}, f32[1,6,8,128]{3,2,1,0:T(8,128)}, f32[1,6,8,128]{3,2,1,0:T(8,128)}) fusion(f32[3,6,8,128]{3,2,1,0:T(8,128)S(1)} %shard_map.58), kind=kLoop, calls=%fused_computation | loop fusion | bytes 147456 | tf_op jit(solution)/shard_map/slice | solution.py:458

commit v3 on v2

--- a/solution.py
+++ b/solution.py
@@ -18,6 +18,7 @@
 SUM_ROWS = 16
 HALF_ROWS = 8
 TILE_I = 256
+AHEAD = 1
 
 
 def group_size(count):
@@ -26,6 +27,10 @@
         if count % size == 0 and size * size <= count:
             best = size
     return best
+
+
+def tile_chunks(chunks):
+    return TILE_I // 128 if chunks % (TILE_I // 128) == 0 else 1
 
 
 def split3(value):
@@ -71,10 +76,10 @@
     out_ref,
     state_ref, mass_ref, freq_ref,
     lhs, weigh, rhs_r, rhs_c, sum_s, sum_t,
-    rows, got, got_mass, grp, tot, carry_in,
+    rows, got, got_mass, own_term, col_in, note, note_in,
     in_sem,
     body_send, body_recv, mass_send, mass_recv,
-    grp_send, grp_recv, tot_send, tot_recv, entered,
+    col_send, col_recv, note_send, note_recv, entered,
 ):
     slot = lax.axis_index("tm")
     half = lax.axis_index("body")
@@ -83,8 +88,9 @@
     r = slot % g
     chunks = state_ref.shape[1]
     lanes = chunks * 128
-    wide = TILE_I // 128 if chunks % (TILE_I // 128) == 0 else 1
+    wide = tile_chunks(chunks)
     span = wide * 128
+    squares = range(chunks // wide)
     touched = set()
     mass_scale = disc_mass / (lanes * nb)
 
@@ -173,8 +179,8 @@
         for c in range(8):
             rows[turn, :, c, :] = order[c]
 
-    def prepare_source(block, ref, mass):
-        for s in range(chunks):
+    def prepare_source(block, ref, mass, square):
+        for s in range(square * wide, (square + 1) * wide):
             body = ref[s]
             high, middle, low = split3(body)
             first = jnp.where(free_row, 1.0, high)
@@ -188,8 +194,8 @@
                 heavy, axis=0
             ).astype(BF16)
 
-    def prepare_target(ref):
-        for s in range(chunks):
+    def prepare_target(ref, square):
+        for s in range(square * wide, (square + 1) * wide):
             body = ref[s]
             high, middle, low = split3(to_dist * body + soften)
             one = jnp.where(norm_row, 1.0, high)
@@ -204,13 +210,32 @@
                 [one, middle, low, one, cross, one], axis=0
             ).astype(BF16)
 
-    def visit(tiles):
+    def visit(turn, tiles, done):
+        built = set()
+
+        def build(tile):
+            block, at, n = tile
+            if block > 0 and (block,) not in built:
+                body_copy(turn, block).wait_recv()
+                if turn == 0:
+                    mass_copy(block).wait_recv()
+            if (block, at) not in built:
+                if block == 0:
+                    prepare_source(0, rows.at[turn], mass_ref, at)
+                else:
+                    prepare_source(
+                        block, got.at[turn, block - 1], got_mass.at[block - 1], at
+                    )
+            if ("target", n) not in built:
+                prepare_target(rows.at[turn], n)
+            built.update([(block,), (block, at), ("target", n)])
+
         def pair(tile):
             block, at, n = tile
-            rows = lhs[block, at * span : (at + 1) * span, :]
+            source = lhs[block, at * span : (at + 1) * span, :]
             cols = slice(n * span, (n + 1) * span)
-            dist = jnp.dot(rows, rhs_r[:, cols], preferred_element_type=F32)
-            closing = jnp.dot(rows, rhs_c[:, cols], preferred_element_type=F32)
+            dist = jnp.dot(source, rhs_r[:, cols], preferred_element_type=F32)
+            closing = jnp.dot(source, rhs_c[:, cols], preferred_element_type=F32)
             return dist, closing
 
         def curve(dist, closing):
@@ -248,17 +273,38 @@
             if block == 0 and at != n:
                 collect(block, n, at, parts, ((1,), (1,)))
 
+        for tile in tiles[: AHEAD + 1]:
+            build(tile)
         ready, parts = pair(tiles[0]), None
-        for index in range(len(tiles)):
+        for index, tile in enumerate(tiles):
             now = ready
+            if index + AHEAD + 1 < len(tiles):
+                build(tiles[index + AHEAD + 1])
             if index + 1 < len(tiles):
                 ready = pair(tiles[index + 1])
             if index > 0:
                 gather(tiles[index - 1], parts)
+                done(index - 1)
             parts = curve(*now)
         gather(tiles[-1], parts)
-
-    def forces(turn, planes):
+        done(len(tiles) - 1)
+
+    def pulls(planes):
+        places, speeds = planes[:3], planes[3:]
+        total, turned = sum_s[:, 3, :], sum_t[:, 3, :]
+        inverse = lax.rsqrt(plane_sum(places, places))
+        cube = inverse * inverse * inverse
+        pull = 3.0 * plane_sum(places, speeds) * inverse * inverse
+        acc, jerk = [], []
+        for c in range(3):
+            p, v = places[c], speeds[c]
+            acc.append(sum_s[:, c, :] - p * total - cube * p)
+            spin = sum_s[:, 4 + c, :] - v * total
+            spin = spin - 3.0 * (sum_t[:, c, :] - p * turned)
+            jerk.append(spin - cube * (v - pull * p))
+        return acc, jerk
+
+    def visits(turn, planes, done):
         publish(turn, planes)
         if turn == 0:
             meet_partner()
@@ -266,47 +312,38 @@
             body_copy(turn, k).start()
             if turn == 0:
                 mass_copy(k).start()
-        prepare_source(0, rows.at[turn], mass_ref)
-        prepare_target(rows.at[turn])
         touched.clear()
-        squares = range(chunks // wide)
-        visit([(0, at, n) for n in squares for at in squares if at >= n])
-        for k in range(1, nb):
-            body_copy(turn, k).wait_recv()
-            if turn == 0:
-                mass_copy(k).wait_recv()
-            prepare_source(k, got.at[turn, k - 1], got_mass.at[k - 1])
-            visit([(k, at, n) for n in squares for at in squares])
-
-        def summed(ref, c):
-            return ref[:, c, :]
-
-        places, speeds = planes[:3], planes[3:]
-        total, turned = summed(sum_s, 3), summed(sum_t, 3)
-        inverse = lax.rsqrt(plane_sum(places, places))
-        cube = inverse * inverse * inverse
-        pull = 3.0 * plane_sum(places, speeds) * inverse * inverse
-        acc, jerk = [], []
-        for c in range(3):
-            p, v = places[c], speeds[c]
-            acc.append(summed(sum_s, c) - p * total - cube * p)
-            spin = summed(sum_s, 4 + c) - v * total
-            spin = spin - 3.0 * (summed(sum_t, c) - p * turned)
-            jerk.append(spin - cube * (v - pull * p))
-        return acc, jerk
+        visit(turn, tiles, done)
+
+    def forces(turn, planes):
+        visits(turn, planes, lambda index: None)
+        return pulls(planes)
+
+    tiles = [(0, at, n) for n in squares for at in squares if at >= n]
+    tiles += [(k, at, n) for k in range(1, nb) for n in squares for at in squares]
 
     for copy in arrivals:
         copy.wait()
     planes = load_planes(state_ref)
     h = fine_step
-    acc, jerk = forces(0, planes)
-    for step in range(2):
+    freq = freq_ref[...]
+    angle = freq * slice_time
+    cos1, sin1 = jnp.cos(angle), jnp.sin(angle)
+    angle_g = float(g) * freq * slice_time
+    cosg, sing = jnp.cos(angle_g), jnp.sin(angle_g)
+    own = planes
+    coarse = drift(own, cos1, sin1, freq)
+    first = slot == 0
+
+    def predict(planes, acc, jerk):
         pos, vel = planes[:3], planes[3:]
-        guess = tuple(
+        return tuple(
             p + h * v + h * h / 2.0 * a + h**3 / 6.0 * j
             for p, v, a, j in zip(pos, vel, acc, jerk)
         ) + tuple(v + h * a + h * h / 2.0 * j for v, a, j in zip(vel, acc, jerk))
-        na, nj = forces(step + 1, guess)
+
+    def correct(planes, acc, jerk, na, nj):
+        pos, vel = planes[:3], planes[3:]
         new_vel = tuple(
             vel[c] + h / 2.0 * (acc[c] + na[c]) + h * h / 12.0 * (jerk[c] - nj[c])
             for c in range(3)
@@ -315,93 +352,129 @@
             pos[c] + h / 2.0 * (vel[c] + new_vel[c]) + h * h / 12.0 * (acc[c] - na[c])
             for c in range(3)
         )
-        planes, acc, jerk = new_pos + new_vel, na, nj
-        if step == 0:
-            meet_slices()
-
-    freq = freq_ref[...]
-    angle = freq * slice_time
-    cos1, sin1 = jnp.cos(angle), jnp.sin(angle)
-    fine = planes
-    own = load_planes(state_ref)
-    coarse = drift(own, cos1, sin1, freq)
-    corr = tuple(a - b for a, b in zip(fine, coarse))
-    first = slot == 0
-    store_planes(grp.at[r], tuple(jnp.where(first, a, b) for a, b in zip(fine, corr)))
-    store_planes(out_ref.at[0], fine)
-    store_planes(out_ref.at[1], corr)
-
-    def grp_copy(k):
+        return new_pos + new_vel
+
+    acc, jerk = forces(0, planes)
+    guess = predict(planes, acc, jerk)
+    na, nj = forces(1, guess)
+    planes, acc, jerk = correct(planes, acc, jerk, na, nj), na, nj
+    meet_slices()
+    guess = predict(planes, acc, jerk)
+
+    def col_copy(part, k):
         return pltpu.make_async_remote_copy(
-            src_ref=grp.at[r], dst_ref=grp.at[r],
-            send_sem=grp_send.at[k - 1], recv_sem=grp_recv.at[r],
-            device_id={"tm": q * g + (r + k) % g},
-        )
-
-    def grp_arrival(k):
-        source = (r + g - k) % g
+            src_ref=own_term.at[part, :, spans[part]],
+            dst_ref=col_in.at[part, k - 1, :, spans[part]],
+            send_sem=col_send.at[part, k - 1], recv_sem=col_recv.at[part, k - 1],
+            device_id={"tm": ((q + k) % ng) * g + r},
+        )
+
+    def note_copy(part, k):
         return pltpu.make_async_remote_copy(
-            src_ref=grp.at[source], dst_ref=grp.at[source],
-            send_sem=grp_send.at[k - 1], recv_sem=grp_recv.at[source],
-            device_id={"tm": q * g + (r + k) % g},
-        )
-
-    for k in range(1, g):
-        grp_copy(k).start()
-    angle_g = float(g) * freq * slice_time
-    cosg, sing = jnp.cos(angle_g), jnp.sin(angle_g)
-    for k in range(1, g):
-        grp_arrival(k).wait_recv()
-
-    def tot_copy(k):
-        return pltpu.make_async_remote_copy(
-            src_ref=tot, dst_ref=carry_in.at[k - 1],
-            send_sem=tot_send.at[k - 1], recv_sem=tot_recv.at[k - 1],
-            device_id={"tm": ((q + k) % ng) * g + r},
-        )
-
-    if ng > 1:
-        value = load_planes(grp.at[0])
-        for m in range(1, g):
-            moved = drift(value, cos1, sin1, freq)
-            value = tuple(a + b for a, b in zip(moved, load_planes(grp.at[m])))
-        store_planes(tot, value)
+            src_ref=note.at[part, k - 1, :, spans[part]],
+            dst_ref=note_in.at[part, k - 1, :, spans[part]],
+            send_sem=note_send.at[part, k - 1], recv_sem=note_recv.at[part, k - 1],
+            device_id={"tm": q * g + (r + g - k) % g},
+        )
+
+    parts = [list(squares)[:-2], *([n] for n in list(squares)[-2:])]
+    parts = [group for group in parts if group]
+    spans = [
+        pl.ds(group[0] * wide, len(group) * wide) for group in parts
+    ]
+    result = {}
+
+    def finish(part):
+        na, nj = pulls(guess)
+        fine = correct(planes, acc, jerk, na, nj)
+        corr = tuple(a - b for a, b in zip(fine, coarse))
+        term = tuple(jnp.where(first, a, b) for a, b in zip(fine, corr))
+        store_planes(own_term.at[part], term)
         for k in range(1, ng):
             @pl.when(q + k < ng)
             def _(k=k):
-                tot_copy(k).start()
-
-    value = tuple(jnp.zeros_like(freq) for _ in range(6))
-    for k in range(ng - 1, 0, -1):
-        @pl.when(k <= q)
-        def _(k=k):
-            tot_copy(k).wait_recv()
-
-        here = k <= q
+                col_copy(part, k).start()
+
+        result["last"] = fine, corr, term
+
+    final = [max(i for i, tile in enumerate(tiles) if tile[2] in group) for group in parts]
+    if nb == 1:
+        final = [len(tiles) - 1] * len(parts)
+
+    def done(index):
+        for part in range(len(parts)):
+            if final[part] == index:
+                finish(part)
+
+    visits(2, guess, done)
+    fine, corr, term = result["last"]
+    store_planes(out_ref.at[0], fine)
+    store_planes(out_ref.at[1], corr)
+
+    before = []
+    for part in range(len(parts)):
+        value = tuple(jnp.zeros_like(freq) for _ in range(6))
+        for k in range(ng - 1, 0, -1):
+            @pl.when(k <= q)
+            def _(k=k):
+                col_copy(part, k).wait_recv()
+
+            here = k <= q
+            moved = drift(value, cosg, sing, freq)
+            value = tuple(
+                jnp.where(here, a + b, c)
+                for a, b, c in zip(moved, load_planes(col_in.at[part, k - 1]), value)
+            )
+        before.append(value)
         moved = drift(value, cosg, sing, freq)
-        value = tuple(
-            jnp.where(here, a + b, c)
-            for a, b, c in zip(moved, load_planes(carry_in.at[k - 1]), value)
-        )
-    for m in range(g - 1):
-        here = m < r
-        moved = drift(value, cos1, sin1, freq)
-        value = tuple(
-            jnp.where(here, a + b, c)
-            for a, b, c in zip(moved, load_planes(grp.at[m]), value)
-        )
-    store_planes(out_ref.at[2], tuple(jnp.where(first, a, b) for a, b in zip(own, value)))
+        after = tuple(a + b for a, b in zip(moved, term))
+        for k in range(1, g):
+            up = r >= k
+            store_planes(
+                note.at[part, k - 1],
+                tuple(jnp.where(up, a, b) for a, b in zip(value, after)),
+            )
+
+            @pl.when((r < k) | (q > 0))
+            def _(k=k):
+                note_copy(part, k).start()
+
+    ahead = own
+    place = lax.broadcasted_iota(jnp.int32, freq.shape, 0)
+    for part in range(len(parts)):
+        value = before[part]
+        for k in range(1, g):
+            here = (r + k >= g) | (q > 0)
+
+            @pl.when(here)
+            def _(k=k):
+                note_copy(part, k).wait_recv()
+
+            moved = drift(value, cos1, sin1, freq)
+            value = tuple(
+                jnp.where(here, a + b, a)
+                for a, b in zip(moved, load_planes(note_in.at[part, k - 1]))
+            )
+        low = parts[part][0] * wide
+        inside = (place >= low) & (place < low + len(parts[part]) * wide)
+        inside = inside & jnp.logical_not(first)
+        ahead = tuple(jnp.where(inside, a, b) for a, b in zip(value, ahead))
+    store_planes(out_ref.at[2], ahead)
 
     for k in range(1, nb):
         mass_copy(k).wait_send()
         for turn in range(3):
             body_copy(turn, k).wait_send()
-    for k in range(1, g):
-        grp_copy(k).wait_send()
-    for k in range(1, ng):
-        @pl.when(q + k < ng)
-        def _(k=k):
-            tot_copy(k).wait_send()
+    for part in range(len(parts)):
+        for k in range(1, ng):
+            @pl.when(q + k < ng)
+            def _(k=k):
+                col_copy(part, k).wait_send()
+
+        for k in range(1, g):
+            @pl.when((r < k) | (q > 0))
+            def _(k=k):
+                note_copy(part, k).wait_send()
 
 
 def solution(mesh):
@@ -413,6 +486,8 @@
     def local(states, masses, frequency):
         lanes = states.shape[2]
         s = lanes // 128
+        wide = tile_chunks(s)
+        tiles = s // wide
         dma = pltpu.SemaphoreType.DMA
         anywhere = pl.BlockSpec(memory_space=pl.ANY)
         outs = pl.pallas_call(
@@ -433,18 +508,19 @@
                 pltpu.VMEM((3, s, 8, 128), F32),
                 pltpu.VMEM((3, max(nb - 1, 1), s, 8, 128), F32),
                 pltpu.VMEM((max(nb - 1, 1), s, 128), F32),
-                pltpu.VMEM((g, 6, s, 128), F32),
-                pltpu.VMEM((6, s, 128), F32),
-                pltpu.VMEM((max(ng - 1, 1), 6, s, 128), F32),
+                pltpu.VMEM((tiles, 6, s, 128), F32),
+                pltpu.VMEM((tiles, max(ng - 1, 1), 6, s, 128), F32),
+                pltpu.VMEM((tiles, max(g - 1, 1), 6, s, 128), F32),
+                pltpu.VMEM((tiles, max(g - 1, 1), 6, s, 128), F32),
                 dma((3,)),
                 dma((3, max(nb - 1, 1))),
                 dma((3, max(nb - 1, 1))),
                 dma((max(nb - 1, 1),)),
                 dma((max(nb - 1, 1),)),
-                dma((max(g - 1, 1),)),
-                dma((g,)),
-                dma((max(ng - 1, 1),)),
-                dma((max(ng - 1, 1),)),
+                dma((tiles, max(ng - 1, 1))),
+                dma((tiles, max(ng - 1, 1))),
+                dma((tiles, max(g - 1, 1))),
+                dma((tiles, max(g - 1, 1))),
                 pltpu.SemaphoreType.REGULAR((2,)),
             ],
             compiler_params=pltpu.CompilerParams(

time: 22.2 us -> 21.4 us (0.964)
  the two profiles are of different devices: /device:TPU:0 before, /device:TPU:24 now
where the time goes in v3:
time: 21.4 us; the launch traced here: 21.2 us
  Pallas kernels  19.9 us (93%)
  between operations  0.64 us (3%)
  local copies, waits for them, and re-layouts  0.63 us (3%)
    pallas_call x1, Pallas kernels, local(): pl.pallas_call(functools.partial(kernel, nt, nb, g), out_shape=pltpu.VMEM...  19.9 us
    slice x1, local copies, waits for them, and re-layouts, local(): return tuple((outs[n].reshape(1, 6, lanes) for n in range(3)))  0.63 us

profile of v3, /device:TPU:24, one launch (start us, length us, event | category | flops | bytes accessed | tf_op | source)
XLA Modules:
  0.0 21.2 jit_solution(16520996444620951282)
XLA Ops:
  0.6 19.9 %shard_map.58 = f32[3,6,8,128]{3,2,1,0:T(8,128)S(1)} custom-call(f32[6,8,128]{2,1,0:T(8,128)} %bitcast.9, f32[8,128]{1,0:T(8,128)} %bitcast.10, f32[8,128]{1,0:T(8,128)} %bitcast.11), custom_call_target="tpu_custom_call" | custom-call | tf_op jit(solution)/shard_map/pallas_call | solution.py:493
  20.6 0.6 %fusion = (f32[1,6,8,128]{3,2,1,0:T(8,128)}, f32[1,6,8,128]{3,2,1,0:T(8,128)}, f32[1,6,8,128]{3,2,1,0:T(8,128)}) fusion(f32[3,6,8,128]{3,2,1,0:T(8,128)S(1)} %shard_map.58), kind=kLoop, calls=%fused_computation | loop fusion | bytes 147456 | tf_op jit(solution)/shard_map/slice | solution.py:534

commit v4 on v3

--- a/solution.py
+++ b/solution.py
@@ -428,7 +428,7 @@
         before.append(value)
         moved = drift(value, cosg, sing, freq)
         after = tuple(a + b for a, b in zip(moved, term))
-        for k in range(1, g):
+        for k in range(g - 1, 0, -1):
             up = r >= k
             store_planes(
                 note.at[part, k - 1],

time: 21.4 us -> 21.4 us (level)
  no operation moved by 1% of the time
where the time goes in v4:
time: 21.4 us; the launch traced here: 21.1 us
  Pallas kernels  19.9 us (93%)
  between operations  0.64 us (3%)
  local copies, waits for them, and re-layouts  0.63 us (3%)
    pallas_call x1, Pallas kernels, local(): pl.pallas_call(functools.partial(kernel, nt, nb, g), out_shape=pltpu.VMEM...  19.9 us
    slice x1, local copies, waits for them, and re-layouts, local(): return tuple((outs[n].reshape(1, 6, lanes) for n in range(3)))  0.63 us

profile of v4, /device:TPU:24, one launch (start us, length us, event | category | flops | bytes accessed | tf_op | source)
XLA Modules:
  0.0 21.1 jit_solution(16369849644758633353)
XLA Ops:
  0.6 19.9 %shard_map.58 = f32[3,6,8,128]{3,2,1,0:T(8,128)S(1)} custom-call(f32[6,8,128]{2,1,0:T(8,128)} %bitcast.9, f32[8,128]{1,0:T(8,128)} %bitcast.10, f32[8,128]{1,0:T(8,128)} %bitcast.11), custom_call_target="tpu_custom_call" | custom-call | tf_op jit(solution)/shard_map/pallas_call | solution.py:493
  20.5 0.6 %fusion = (f32[1,6,8,128]{3,2,1,0:T(8,128)}, f32[1,6,8,128]{3,2,1,0:T(8,128)}, f32[1,6,8,128]{3,2,1,0:T(8,128)}) fusion(f32[3,6,8,128]{3,2,1,0:T(8,128)S(1)} %shard_map.58), kind=kLoop, calls=%fused_computation | loop fusion | bytes 147456 | tf_op jit(solution)/shard_map/slice | solution.py:534
